TPU v7x, 32 devices: a whole 2x2x4 slice. The times are simulated.
32 devices in a mesh: parts: 2 (over y), seq: 4 (over z), chan: 4 (over x, core).
Axes of the slice: x: 2, y: 2, z: 4, core: 2. Of those that a mesh axis runs over, the one named last changes fastest.
Arguments:
- records: bfloat16 [8, 1536, 512], P('parts', 'seq', 'chan'), parts along dimension 0, may hold values from -6 to 6
- norm_gain: float32 [512], replicated, may hold values from 0.1 to 1.9
- in_projection: bfloat16 [512, 3, 512], P(None, None, 'chan'), may hold values from -0.25 to 0.25
- short_kernel: float32 [3, 3, 512], P(None, None, 'chan'), may hold values from -3.5 to 3.5
- long_filter: bfloat16 [16, 1536], P('chan', 'seq'), may hold values from -1.6 to 1.6
- skip_gain: float32 [512], P('chan'), may hold values from 0.5 to 1.5
- out_projection: bfloat16 [512, 512], P('chan'), may hold values from -0.25 to 0.25
Outputs:
- mixed: bfloat16 [8, 1536, 512], P('parts', 'seq', 'chan'), parts along dimension 0
There are 2 independent parts, one for each index of `parts`. A program takes and returns all parts, laid end to end along the dimension named above; an argument that names none is the same for every part. Nothing has to cross between parts.
All inputs are finite; a program needn't handle non-finite values.
Results may differ from a plain program's by a relative error of at most 0.015.
Values may be sent and summed in bfloat16 or wider, within the bound.
A program may use at most 128 MiB of HBM per device.

v0:
```python
import jax
import jax.numpy as jnp
from jax import lax
from jax.sharding import PartitionSpec as P


def from_behind(block, axis, distance):
    devices = range(lax.axis_size(axis))
    route = [(i - distance, i) for i in devices if i - distance in devices]
    return lax.ppermute(block, axis, route)


def block_terms(taps_padded, offset, block_source, block_len):
    filter_count = taps_padded.shape[0]
    window = lax.dynamic_slice_in_dim(taps_padded, offset + 1, 2 * block_len - 1, 1)
    flipped = window[:, ::-1]
    padded = jnp.pad(flipped, ((0, 0), (0, 1)))
    tiled_taps = jnp.tile(padded, (1, block_len))
    toeplitz = tiled_taps[:, block_len - 1 : block_len - 1 + block_len * (2 * block_len - 1)]
    toeplitz = toeplitz.reshape(filter_count, block_len, 2 * block_len - 1)[:, :, :block_len]
    record_count = block_source.shape[0]
    grouped = block_source.reshape(record_count, block_len, filter_count, -1)
    return jnp.einsum("fab,rbfg->rafg", toeplitz, grouped, preferred_element_type=jnp.float32)


def body(records, norm_gain, in_projection, short_kernel, long_filter, skip_gain, out_projection):
    gathered = lax.all_gather(records, "chan", axis=2, tiled=True)
    widened = gathered.astype(jnp.float32)
    inv_rms = lax.rsqrt(jnp.mean(widened * widened, axis=-1, keepdims=True) + 1e-06)
    normed = (widened * inv_rms * norm_gain).astype(jnp.bfloat16)
    projected = jnp.einsum(
        "rtd,dkc->rtkc", normed, in_projection, preferred_element_type=jnp.float32
    ).astype(jnp.bfloat16)
    rim_rows = from_behind(projected[:, -2:], "seq", 1)
    extended = jnp.concatenate([rim_rows, projected], axis=1).astype(jnp.float32)
    streams = (
        short_kernel[0] * extended[:, 2:]
        + short_kernel[1] * extended[:, 1:-1]
        + short_kernel[2] * extended[:, :-2]
    )
    query_gate = streams[:, :, 0]
    gated_source = (streams[:, :, 1] * streams[:, :, 2]).astype(jnp.bfloat16)
    record_count = gated_source.shape[0]
    block_len = gated_source.shape[1]
    channels = gated_source.shape[2]
    all_taps = lax.all_gather(long_filter, "seq", axis=1, tiled=True)
    taps_padded = jnp.concatenate(
        [jnp.zeros((all_taps.shape[0], block_len), jnp.bfloat16), all_taps], axis=1
    )
    my_start = lax.axis_index("seq") * block_len
    cycle_stops = lax.axis_size("seq")
    long_sum = block_terms(taps_padded, 0, gated_source, block_len)

    def advance(stop_index, state):
        running_sum, visiting = state
        visiting = from_behind(visiting, "seq", 1)
        lag_start = stop_index * block_len
        running_sum = lax.cond(
            lag_start <= my_start,
            lambda running: running + block_terms(taps_padded, lag_start, visiting, block_len),
            lambda running: running,
            running_sum,
        )
        return (running_sum, visiting)

    long_sum, visiting = lax.fori_loop(1, cycle_stops, advance, (long_sum, gated_source))
    long_out = long_sum.reshape(
        record_count, block_len, channels
    ) + skip_gain * gated_source.astype(jnp.float32)
    gated = (query_gate * long_out).astype(jnp.bfloat16)
    partial_terms = jnp.einsum(
        "rtc,cd->rtd", gated, out_projection, preferred_element_type=jnp.float32
    )
    return lax.psum_scatter(
        partial_terms.astype(jnp.bfloat16), "chan", scatter_dimension=2, tiled=True
    )


def solution(mesh):
    placed = (
        P("parts", "seq", "chan"),
        P(),
        P(None, None, "chan"),
        P(None, None, "chan"),
        P("chan", "seq"),
        P("chan"),
        P("chan", None),
    )
    return jax.shard_map(
        body, mesh=mesh, in_specs=placed, out_specs=P("parts", "seq", "chan"), check_vma=False
    )
```

profile of v0, /device:TPU:0, one launch (start us, length us, event | category | flops | bytes accessed | tf_op | source)
XLA Modules:
  0.0 202.3 jit_solution(438159001702864460)
XLA Ops:
  6.5 0.7 all-gather.2.cloned.1.call-update
  7.3 0.0 reduce-scatter.4.cloned.1.call-start
  7.3 14.9 %all_gather.7 = bf16[4,1536]{1,0:T(4,128)(2,1)S(1)} all-gather(bf16[4,384]{1,0:T(4,128)(2,1)} %param.15), channel_id=1, replica_groups=mesh['parts'=2,'seq'=4,'chan'=4] {'seq'}, dimensions={1}, use_global_device_ids=true | all-gather | bytes 15360 | tf_op jit(solution)/shard_map/all_gather | solution.py:46
  22.2 0.1 pad_slice_fusion
  22.2 0.5 reverse.1
  22.8 0.1 slice.94
  22.9 0.2 broadcast_bitcast_fusion.1
  23.0 8.4 %all-gather.2.cloned.1.call-done = bf16[4,384,512]{2,1,0:T(8,128)(2,1)} async-done(((bf16[4,384,128]{2,1,0:T(8,128)(2,1)}), bf16[4,384,512]{2,1,0:T(8,128)(2,1)}) %all-gather.2.cloned.1.call-update) | async-done | bytes 1572880 | tf_op jit(solution)/shard_map/all_gather | solution.py:27
  31.5 1.8 fusion.2
  33.3 0.0 copy-done
  33.3 0.0 copy-done.9
  33.3 0.0 copy-start.7
  33.3 2.4 %fusion.12 = bf16[4,384,3,128]{3,1,2,0:T(8,128)(2,1)S(1)} fusion(bf16[4,384,512]{2,1,0:T(8,128)(2,1)} %all-gather.2.cloned.1.call-done, f32[512]{0:T(512)S(1)} %copy-done.9, f32[4,384]{1,0:T(4,128)S(1)} %add_rsqrt_fusion, bf16[512,3,128]{2,0,1:T(8,128)(2,1)S(1)} %copy-done), kind=kOutput, calls=%fused_computation.19 | convolution fusion | flops 607715328 | bytes 3153920 | tf_op jit(solution)/shard_map/rtd,dkc->rtkc/dot_general | solution.py:31
  35.8 0.0 copy-start.5
  35.8 3.4 %collective-permute-start.1 = (bf16[4,2,3,128]{3,1,2,0:T(2,128)(2,1)S(1)}, bf16[4,2,3,128]{3,1,2,0:T(2,128)(2,1)S(1)}, u32[]{:S(2)}, u32[]{:S(2)}) collective-permute-start(bf16[4,2,3,128]{3,1,2,0:T(2,128)(2,1)S(1)} %slice.56), channel_id=1, source_target_pairs={{0,4},{4,8},{8,12},{1,5},{5,9},{9,13},{2,6},{6,10},{10,14},{3,7},{... | collective-permute-start | bytes 18440 | tf_op jit(solution)/shard_map/ppermute | solution.py:10
  39.2 1.8 copy.32
  41.1 2.8 %slice.63 = bf16[4,294528]{1,0:T(4,128)(2,1)} slice(bf16[4,294912]{1,0:T(4,128)(2,1)S(1)} %bitcast.67), slice={[0:4], [383:294911]} | slice | bytes 4712448 | tf_op jit(solution)/shard_map/slice | solution.py:19
  43.9 3.3 %reshape.52 = bf16[1178112]{0:T(1024)(128)(2,1)S(1)} reshape(bf16[4,294528]{1,0:T(4,128)(2,1)} %slice.63) | data formatting | bytes 4712448
  47.2 6.5 %reshape.40 = bf16[4,384,767]{2,1,0:T(8,128)(2,1)} reshape(bf16[1178112]{0:T(1024)(128)(2,1)S(1)} %reshape.52) | data formatting | bytes 4712448 | tf_op jit(solution)/shard_map/reshape | solution.py:20
  53.7 0.0 collective-permute-done.1
  53.7 1.5 maximum_convert_fusion
  55.2 0.7 fusion.5
  55.9 0.1 fusion.15
  56.0 1.3 copy-done.1
  57.3 0.8 fusion.25
  58.1 0.2 copy.21
  58.4 1.9 copy.23
  60.3 1.4 convolution_bitcast_fusion
  61.7 57.2 %while.18 = (s32[]{:T(128)}, f32[4,384,4,32]{1,3,0,2:T(8,128)}, bf16[4,384,128]{1,2,0:T(8,128)(2,1)}, s32[]{:T(128)}, bf16[4,1920]{1,0:T(4,128)(2,1)S(1)}, /*index=5*/s32[]{:T(128)}, s32[]{:T(128)}) while((s32[]{:T(128)}, f32[4,384,4,32]{1,3,0,2:T(8,128)}, bf16[4,384,128]{1,2,0:T(8,128)(2,1)}, s32[]{:T(128)}, bf16[4,1920]{1,0:T(4,128)(2,1)S(1)}, ...), condition=%wide.region_4.5_spmd, body=%wide.region_1.4_spmd.sunk | while | flops 151191552 | bytes 29135044 | solution.py:66
  61.7 3.4 %collective-permute-start = (bf16[4,384,128]{1,2,0:T(8,128)(2,1)}, bf16[4,384,128]{1,2,0:T(8,128)(2,1)S(1)}, u32[]{:S(2)}, u32[]{:S(2)}) collective-permute-start(bf16[4,384,128]{1,2,0:T(8,128)(2,1)} %get-tuple-element.183), channel_id=1, source_target_pairs={{0,4},{4,8},{8,12},{1,5},{5,9},{9,13},{2,6},{6,10},{10,14},{3,7},{... | collective-permute-start | bytes 1179656 | tf_op jit(solution)/shard_map/while/body/eval_jaxpr/ppermute | solution.py:10
  65.1 8.8 %collective-permute-done = bf16[4,384,128]{1,2,0:T(8,128)(2,1)S(1)} collective-permute-done((bf16[4,384,128]{1,2,0:T(8,128)(2,1)}, bf16[4,384,128]{1,2,0:T(8,128)(2,1)S(1)}, u32[]{:S(2)}, u32[]{:S(2)}) %collective-permute-start) | collective-permute-done | bytes 393248 | tf_op jit(solution)/shard_map/while/body/eval_jaxpr/ppermute | solution.py:10
  73.9 0.8 copy.46
  74.7 23.5 %collective-permute-start = (bf16[4,384,128]{1,2,0:T(8,128)(2,1)}, bf16[4,384,128]{1,2,0:T(8,128)(2,1)S(1)}, u32[]{:S(2)}, u32[]{:S(2)}) collective-permute-start(bf16[4,384,128]{1,2,0:T(8,128)(2,1)} %get-tuple-element.183), channel_id=1, source_target_pairs={{0,4},{4,8},{8,12},{1,5},{5,9},{9,13},{2,6},{6,10},{10,14},{3,7},{... | collective-permute-start | bytes 1179656 | tf_op jit(solution)/shard_map/while/body/eval_jaxpr/ppermute | solution.py:10
  98.2 7.9 %collective-permute-done = bf16[4,384,128]{1,2,0:T(8,128)(2,1)S(1)} collective-permute-done((bf16[4,384,128]{1,2,0:T(8,128)(2,1)}, bf16[4,384,128]{1,2,0:T(8,128)(2,1)S(1)}, u32[]{:S(2)}, u32[]{:S(2)}) %collective-permute-start) | collective-permute-done | bytes 393248 | tf_op jit(solution)/shard_map/while/body/eval_jaxpr/ppermute | solution.py:10
  106.1 0.8 copy.46
  106.9 4.3 %collective-permute-start = (bf16[4,384,128]{1,2,0:T(8,128)(2,1)}, bf16[4,384,128]{1,2,0:T(8,128)(2,1)S(1)}, u32[]{:S(2)}, u32[]{:S(2)}) collective-permute-start(bf16[4,384,128]{1,2,0:T(8,128)(2,1)} %get-tuple-element.183), channel_id=1, source_target_pairs={{0,4},{4,8},{8,12},{1,5},{5,9},{9,13},{2,6},{6,10},{10,14},{3,7},{... | collective-permute-start | bytes 1179656 | tf_op jit(solution)/shard_map/while/body/eval_jaxpr/ppermute | solution.py:10
  111.2 7.0 %collective-permute-done = bf16[4,384,128]{1,2,0:T(8,128)(2,1)S(1)} collective-permute-done((bf16[4,384,128]{1,2,0:T(8,128)(2,1)}, bf16[4,384,128]{1,2,0:T(8,128)(2,1)S(1)}, u32[]{:S(2)}, u32[]{:S(2)}) %collective-permute-start) | collective-permute-done | bytes 393248 | tf_op jit(solution)/shard_map/while/body/eval_jaxpr/ppermute | solution.py:10
  118.2 0.8 copy.46
  118.9 1.2 copy.24
  120.2 1.2 copy.25
  121.4 0.0 copy-done.6
  121.4 1.9 convolution_convert_fusion
  123.3 1.4 copy.28
  124.8 1.4 copy.33
  126.2 0.0 reduce-scatter.4.cloned.1.call-update
  126.2 67.1 %reduce-scatter.4.cloned.1.call-done = bf16[128,1536]{1,0:T(8,128)(2,1)} async-done(((bf16[512,1536]{1,0:T(8,128)(2,1)}), bf16[128,1536]{1,0:T(8,128)(2,1)}) %reduce-scatter.4.cloned.1.call-update) | async-done | bytes 393232
  193.4 1.1 reshape.49
  194.4 1.0 copy.29
  (23 shorter events, 0.1 us)
Async XLA Ops:
  6.5 26.8 %copy-start = (bf16[512,3,128]{2,0,1:T(8,128)(2,1)S(1)}, bf16[512,3,128]{2,0,1:T(8,128)(2,1)}, u32[]{:S(2)}) copy-start(bf16[512,3,128]{2,0,1:T(8,128)(2,1)} %param.13) | copy-start | bytes 1179652
  6.5 26.8 %copy-start.9 = (f32[512]{0:T(512)S(1)}, f32[512]{0:T(512)}, u32[]{:S(2)}) copy-start(f32[512]{0:T(512)} %param.12) | copy-start | bytes 6148
  6.5 24.9 %all-gather.2.cloned.1.call-start = ((), (), s32[]{:S(2)}) async-start(), calls=%async_computation.1 | async-start | bytes 1966080 | tf_op jit(solution)/shard_map/all_gather | solution.py:27
  7.3 186.1 %reduce-scatter.4.cloned.1.call-start = ((), (), s32[]{:S(2)}) async-start(), calls=%async_computation.2 | async-start | bytes 1966080
  33.3 5.9 %copy-start.7 = (f32[3,3,128]{2,1,0:T(4,128)S(1)}, f32[3,3,128]{2,1,0:T(4,128)}, u32[]{:S(2)}) copy-start(f32[3,3,128]{2,1,0:T(4,128)} %param.14) | copy-start | bytes 13828
  35.8 3.5 %copy-start.5 = (bf16[4,384,3,128]{3,1,2,0:T(8,128)(2,1)}, bf16[4,384,3,128]{3,1,2,0:T(8,128)(2,1)S(1)}, u32[]{:S(2)}) copy-start(bf16[4,384,3,128]{3,1,2,0:T(8,128)(2,1)S(1)} %fusion.12) | copy-start | bytes 3538948
  35.8 17.9 %collective-permute-start.1 = (bf16[4,2,3,128]{3,1,2,0:T(2,128)(2,1)S(1)}, bf16[4,2,3,128]{3,1,2,0:T(2,128)(2,1)S(1)}, u32[]{:S(2)}, u32[]{:S(2)}) collective-permute-start(bf16[4,2,3,128]{3,1,2,0:T(2,128)(2,1)S(1)} %slice.56), channel_id=1, source_target_pairs={{0,4},{4,8},{8,12},{1,5},{5,9},{9,13},{2,6},{6,10},{10,14},{3,7},{... | collective-permute-start | bytes 18440 | tf_op jit(solution)/shard_map/ppermute | solution.py:10
  55.9 1.4 copy-start.1
  55.9 4.4 %copy-start.2 = (bf16[4,384,767]{2,1,0:T(8,128)(2,1)S(1)}, bf16[4,384,767]{2,1,0:T(8,128)(2,1)}, u32[]{:S(2)}) copy-start(bf16[4,384,767]{2,1,0:T(8,128)(2,1)} %reshape.40) | copy-start | bytes 7068676
  57.3 4.4 %copy-start.3 = (bf16[4,384,1,128]{3,1,2,0:T(8,128)(2,1)}, bf16[4,384,1,128]{3,1,2,0:T(8,128)(2,1)S(1)}, u32[]{:S(2)}) copy-start(bf16[4,384,1,128]{3,1,2,0:T(8,128)(2,1)S(1)} %fusion.15) | copy-start | bytes 1179652
  61.7 12.2 %collective-permute-start = (bf16[4,384,128]{1,2,0:T(8,128)(2,1)}, bf16[4,384,128]{1,2,0:T(8,128)(2,1)S(1)}, u32[]{:S(2)}, u32[]{:S(2)}) collective-permute-start(bf16[4,384,128]{1,2,0:T(8,128)(2,1)} %get-tuple-element.183), channel_id=1, source_target_pairs={{0,4},{4,8},{8,12},{1,5},{5,9},{9,13},{2,6},{6,10},{10,14},{3,7},{... | collective-permute-start | bytes 1179656 | tf_op jit(solution)/shard_map/while/body/eval_jaxpr/ppermute | solution.py:10
  74.7 31.5 %collective-permute-start = (bf16[4,384,128]{1,2,0:T(8,128)(2,1)}, bf16[4,384,128]{1,2,0:T(8,128)(2,1)S(1)}, u32[]{:S(2)}, u32[]{:S(2)}) collective-permute-start(bf16[4,384,128]{1,2,0:T(8,128)(2,1)} %get-tuple-element.183), channel_id=1, source_target_pairs={{0,4},{4,8},{8,12},{1,5},{5,9},{9,13},{2,6},{6,10},{10,14},{3,7},{... | collective-permute-start | bytes 1179656 | tf_op jit(solution)/shard_map/while/body/eval_jaxpr/ppermute | solution.py:10
  106.9 11.3 %collective-permute-start = (bf16[4,384,128]{1,2,0:T(8,128)(2,1)}, bf16[4,384,128]{1,2,0:T(8,128)(2,1)S(1)}, u32[]{:S(2)}, u32[]{:S(2)}) collective-permute-start(bf16[4,384,128]{1,2,0:T(8,128)(2,1)} %get-tuple-element.183), channel_id=1, source_target_pairs={{0,4},{4,8},{8,12},{1,5},{5,9},{9,13},{2,6},{6,10},{10,14},{3,7},{... | collective-permute-start | bytes 1179656 | tf_op jit(solution)/shard_map/while/body/eval_jaxpr/ppermute | solution.py:10
  118.9 2.4 %copy-start.4 = (bf16[4,384,1,128]{3,1,2,0:T(8,128)(2,1)S(1)}, bf16[4,384,1,128]{3,1,2,0:T(8,128)(2,1)}, u32[]{:S(2)}) copy-start(bf16[4,384,1,128]{3,1,2,0:T(8,128)(2,1)} %copy-done.3) | copy-start | bytes 1179652
  118.9 2.4 %copy-start.6 = (bf16[128,512]{1,0:T(8,128)(2,1)S(1)}, bf16[128,512]{1,0:T(8,128)(2,1)}, u32[]{:S(2)}) copy-start(bf16[128,512]{1,0:T(8,128)(2,1)} %param.17) | copy-start | bytes 393220
  118.9 2.4 %copy-start.8 = (f32[128]{0:T(128)S(1)}, f32[128]{0:T(128)}, u32[]{:S(2)}) copy-start(f32[128]{0:T(128)} %param.16) | copy-start | bytes 1540
Sparse Core Ops, SparseCore 0:
  8.9 22.5 all-gather.1
  126.3 66.9 reduce-scatter.3
where the time goes:
time: 203 us; the launch traced here: 202 us
  waiting for transfers between devices  100 us (49%)
  starting transfers between devices  34.6 us (17%)
  local copies, waits for them, and re-layouts  28.4 us (14%)
  blocking collectives  14.9 us (7%)
  between operations  13.6 us (7%)
  matrix products  5.77 us (3%)
  other arithmetic  4.91 us (2%)
    unnamed x3, waiting for transfers between devices  67.9 us
    ppermute x4, starting transfers between devices, from_behind(): return lax.ppermute(block, axis, route)  34.6 us
    ppermute x4, waiting for transfers between devices, from_behind(): return lax.ppermute(block, axis, route)  23.7 us
    all_gather x1, blocking collectives, body(): all_taps = lax.all_gather(long_filter, 'seq', axis=1, tiled=True)  14.9 us
    unnamed x29, local copies, waits for them, and re-layouts  12.2 us
    all_gather x1, waiting for transfers between devices, body(): gathered = lax.all_gather(records, 'chan', axis=2, tiled=True)  8.44 us
    reshape x1, local copies, waits for them, and re-layouts, block_terms(): toeplitz.reshape(filter_count, block_len, 2 * block_len - 1)  6.49 us
  transfers between devices with their start and end apart: 6, of which 5 were waited for; matrix products, arithmetic and copies ran while one was open for 8% of the time, Pallas kernels for 0%

commit v1 on v0

--- a/solution.py
+++ b/solution.py
@@ -2,6 +2,17 @@
 import jax.numpy as jnp
 from jax import lax
 from jax.sharding import PartitionSpec as P
+
+
+def pass_along(array, axis, dim):
+    count = lax.axis_size(axis)
+    hops = [(i, (i + 1) % count) for i in range(count)]
+    pieces = [array]
+    for far in range(1, count):
+        pieces = [lax.ppermute(pieces[0], axis, hops), *pieces]
+    out = jnp.concatenate(pieces, axis=dim)
+    places = (lax.axis_index(axis) + 1) * pieces[-1].shape[dim]
+    return jnp.roll(out, places, axis=dim)
 
 
 def from_behind(block, axis, distance):
@@ -24,7 +35,7 @@
 
 
 def body(records, norm_gain, in_projection, short_kernel, long_filter, skip_gain, out_projection):
-    gathered = lax.all_gather(records, "chan", axis=2, tiled=True)
+    gathered = pass_along(records, "chan", 2)
     widened = gathered.astype(jnp.float32)
     inv_rms = lax.rsqrt(jnp.mean(widened * widened, axis=-1, keepdims=True) + 1e-06)
     normed = (widened * inv_rms * norm_gain).astype(jnp.bfloat16)

time: 203 us -> 202 us (level)
    ppermute x0 -> x3, waiting for transfers between devices: none -> 13.9 us  [pass_along(): pieces = [lax.ppermute(pieces[0], axis, hops), *pieces]]
    all_gather x1 -> x0, waiting for transfers between devices: 8.44 us -> none  [body(): gathered = lax.all_gather(records, 'chan', axis=2, tiled=True)]
    ppermute x4, waiting for transfers between devices: 23.7 us -> 20.8 us  [from_behind(): return lax.ppermute(block, axis, route)]
    unnamed x29 -> x38, local copies, waits for them, and re-layouts: 12.2 us -> 13.1 us
    unnamed x3 -> x2, waiting for transfers between devices: 67.9 us -> 67.6 us
  transfers between devices with their start and end apart: 6 -> 8, of which waited for: 5 -> 6; matrix products, arithmetic and copies ran while one was open for 8% -> 8% of each run, Pallas kernels for 0% -> 0%
where the time goes in v1:
time: 202 us
  waiting for transfers between devices  102 us (50%)
  starting transfers between devices  34.1 us (17%)
  local copies, waits for them, and re-layouts  29.4 us (15%)
  blocking collectives  14.2 us (7%)
  between operations  13.7 us (7%)
  matrix products  4.38 us (2%)
  other arithmetic  3.51 us (2%)
    unnamed x2, waiting for transfers between devices  67.6 us
    ppermute x4, starting transfers between devices, from_behind(): return lax.ppermute(block, axis, route)  33.5 us
    ppermute x4, waiting for transfers between devices, from_behind(): return lax.ppermute(block, axis, route)  20.8 us
    all_gather x1, blocking collectives, body(): all_taps = lax.all_gather(long_filter, 'seq', axis=1, tiled=True)  14.2 us
    ppermute x3, waiting for transfers between devices, pass_along(): pieces = [lax.ppermute(pieces[0], axis, hops), *pieces]  13.9 us
    unnamed x38, local copies, waits for them, and re-layouts  13.1 us
    reshape x1, local copies, waits for them, and re-layouts, block_terms(): toeplitz.reshape(filter_count, block_len, 2 * block_len - 1)  6.48 us
  transfers between devices with their start and end apart: 8, of which 6 were waited for; matrix products, arithmetic and copies ran while one was open for 8% of the time, Pallas kernels for 0%

profile of v1, /device:TPU:0, one launch (start us, length us, event | category | flops | bytes accessed | tf_op | source)
XLA Modules:
  0.0 201.6 jit_solution(10870840893463865665)
XLA Ops:
  6.5 0.5 collective-permute-start.1
  7.0 7.6 %collective-permute-done.1 = bf16[4,384,128]{2,1,0:T(8,128)(2,1)S(1)} collective-permute-done((bf16[4,384,128]{2,1,0:T(8,128)(2,1)}, bf16[4,384,128]{2,1,0:T(8,128)(2,1)S(1)}, u32[]{:S(2)}, u32[]{:S(2)}) %collective-permute-start.1) | collective-permute-done | bytes 393248 | tf_op jit(solution)/shard_map/ppermute | solution.py:12
  14.6 14.2 %all_gather.3 = bf16[4,1536]{1,0:T(4,128)(2,1)S(1)} all-gather(bf16[4,384]{1,0:T(4,128)(2,1)} %param.15), channel_id=1, replica_groups=mesh['parts'=2,'seq'=4,'chan'=4] {'seq'}, dimensions={1}, use_global_device_ids=true | all-gather | bytes 15360 | tf_op jit(solution)/shard_map/all_gather | solution.py:57
  28.9 0.5 reverse.1
  29.5 0.1 slice.94
  29.6 0.2 broadcast_bitcast_fusion.1
  29.7 6.3 %collective-permute-done.3 = bf16[4,384,128]{2,1,0:T(8,128)(2,1)S(1)} collective-permute-done((bf16[4,384,128]{2,1,0:T(8,128)(2,1)S(1)}, bf16[4,384,128]{2,1,0:T(8,128)(2,1)S(1)}, u32[]{:S(2)}, u32[]{:S(2)}) %collective-permute-start.3) | collective-permute-done | bytes 393248 | tf_op jit(solution)/shard_map/ppermute | solution.py:12
  36.0 0.1 constant_dynamic-update-slice_fusion.7
  36.2 0.1 constant_dynamic-update-slice_fusion.6
  36.3 0.1 constant_dynamic-update-slice_fusion.5
  36.4 0.1 constant_dynamic-update-slice_fusion.4
  36.6 0.1 constant_dynamic-update-slice_fusion.3
  36.7 0.1 constant_dynamic-update-slice_fusion.2
  36.9 0.1 constant_dynamic-update-slice_fusion.1
  37.0 0.1 constant_dynamic-update-slice_fusion
  37.2 0.4 fusion.2
  37.6 1.0 fusion.12
  38.7 3.7 %collective-permute-start.4 = (bf16[4,2,3,128]{3,1,2,0:T(2,128)(2,1)S(1)}, bf16[4,2,3,128]{3,1,2,0:T(2,128)(2,1)S(1)}, u32[]{:S(2)}, u32[]{:S(2)}) collective-permute-start(bf16[4,2,3,128]{3,1,2,0:T(2,128)(2,1)S(1)} %slice.56), channel_id=1, source_target_pairs={{0,4},{4,8},{8,12},{1,5},{5,9},{9,13},{2,6},{6,10},{10,14},{3,7},{... | collective-permute-start | bytes 18440 | tf_op jit(solution)/shard_map/ppermute | solution.py:21
  42.4 1.8 copy.32
  44.3 2.8 %slice.63 = bf16[4,294528]{1,0:T(4,128)(2,1)} slice(bf16[4,294912]{1,0:T(4,128)(2,1)S(1)} %bitcast.67), slice={[0:4], [383:294911]} | slice | bytes 4712448 | tf_op jit(solution)/shard_map/slice | solution.py:30
  47.0 3.3 %reshape.52 = bf16[1178112]{0:T(1024)(128)(2,1)S(1)} reshape(bf16[4,294528]{1,0:T(4,128)(2,1)} %slice.63) | data formatting | bytes 4712448
  50.3 6.5 %reshape.40 = bf16[4,384,767]{2,1,0:T(8,128)(2,1)} reshape(bf16[1178112]{0:T(1024)(128)(2,1)S(1)} %reshape.52) | data formatting | bytes 4712448 | tf_op jit(solution)/shard_map/reshape | solution.py:31
  56.8 1.5 maximum_convert_fusion
  58.3 0.7 fusion.5
  59.1 0.1 fusion.16
  59.1 1.3 copy-done.1
  60.5 0.8 fusion.27
  61.3 0.2 copy.21
  61.5 1.9 copy.23
  63.4 1.4 convolution_bitcast_fusion
  64.9 52.9 %while.18 = (s32[]{:T(128)}, f32[4,384,4,32]{1,3,0,2:T(8,128)}, bf16[4,384,128]{1,2,0:T(8,128)(2,1)}, s32[]{:T(128)}, bf16[4,1920]{1,0:T(4,128)(2,1)S(1)}, /*index=5*/s32[]{:T(128)}, s32[]{:T(128)}) while((s32[]{:T(128)}, f32[4,384,4,32]{1,3,0,2:T(8,128)}, bf16[4,384,128]{1,2,0:T(8,128)(2,1)}, s32[]{:T(128)}, bf16[4,1920]{1,0:T(4,128)(2,1)S(1)}, ...), condition=%wide.region_4.5_spmd, body=%wide.region_1.4_spmd.sunk | while | flops 151191552 | bytes 29135044 | solution.py:77
  64.9 1.9 collective-permute-start
  66.8 7.9 %collective-permute-done = bf16[4,384,128]{1,2,0:T(8,128)(2,1)S(1)} collective-permute-done((bf16[4,384,128]{1,2,0:T(8,128)(2,1)}, bf16[4,384,128]{1,2,0:T(8,128)(2,1)S(1)}, u32[]{:S(2)}, u32[]{:S(2)}) %collective-permute-start) | collective-permute-done | bytes 393248 | tf_op jit(solution)/shard_map/while/body/eval_jaxpr/ppermute | solution.py:21
  74.7 0.8 copy.53
  75.5 23.6 %collective-permute-start = (bf16[4,384,128]{1,2,0:T(8,128)(2,1)}, bf16[4,384,128]{1,2,0:T(8,128)(2,1)S(1)}, u32[]{:S(2)}, u32[]{:S(2)}) collective-permute-start(bf16[4,384,128]{1,2,0:T(8,128)(2,1)} %get-tuple-element.183), channel_id=1, source_target_pairs={{0,4},{4,8},{8,12},{1,5},{5,9},{9,13},{2,6},{6,10},{10,14},{3,7},{... | collective-permute-start | bytes 1179656 | tf_op jit(solution)/shard_map/while/body/eval_jaxpr/ppermute | solution.py:21
  99.1 6.9 %collective-permute-done = bf16[4,384,128]{1,2,0:T(8,128)(2,1)S(1)} collective-permute-done((bf16[4,384,128]{1,2,0:T(8,128)(2,1)}, bf16[4,384,128]{1,2,0:T(8,128)(2,1)S(1)}, u32[]{:S(2)}, u32[]{:S(2)}) %collective-permute-start) | collective-permute-done | bytes 393248 | tf_op jit(solution)/shard_map/while/body/eval_jaxpr/ppermute | solution.py:21
  106.0 0.8 copy.53
  106.8 4.3 %collective-permute-start = (bf16[4,384,128]{1,2,0:T(8,128)(2,1)}, bf16[4,384,128]{1,2,0:T(8,128)(2,1)S(1)}, u32[]{:S(2)}, u32[]{:S(2)}) collective-permute-start(bf16[4,384,128]{1,2,0:T(8,128)(2,1)} %get-tuple-element.183), channel_id=1, source_target_pairs={{0,4},{4,8},{8,12},{1,5},{5,9},{9,13},{2,6},{6,10},{10,14},{3,7},{... | collective-permute-start | bytes 1179656 | tf_op jit(solution)/shard_map/while/body/eval_jaxpr/ppermute | solution.py:21
  111.1 6.0 %collective-permute-done = bf16[4,384,128]{1,2,0:T(8,128)(2,1)S(1)} collective-permute-done((bf16[4,384,128]{1,2,0:T(8,128)(2,1)}, bf16[4,384,128]{1,2,0:T(8,128)(2,1)S(1)}, u32[]{:S(2)}, u32[]{:S(2)}) %collective-permute-start) | collective-permute-done | bytes 393248 | tf_op jit(solution)/shard_map/while/body/eval_jaxpr/ppermute | solution.py:21
  117.1 0.8 copy.53
  117.8 1.2 copy.24
  119.1 1.2 copy.25
  120.2 1.9 convolution_convert_fusion
  122.2 1.4 copy.28
  123.6 1.4 copy.33
  125.1 67.6 %reduce-scatter.4.cloned.1.call-done = bf16[128,1536]{1,0:T(8,128)(2,1)} async-done(((bf16[512,1536]{1,0:T(8,128)(2,1)}), bf16[128,1536]{1,0:T(8,128)(2,1)}) %reduce-scatter.4.cloned.1.call-update) | async-done | bytes 393232
  192.7 1.1 reshape.49
  193.8 1.0 copy.29
  (36 shorter events, 0.3 us)
Async XLA Ops:
  6.5 31.0 %copy-start = (bf16[512,3,128]{2,0,1:T(8,128)(2,1)S(1)}, bf16[512,3,128]{2,0,1:T(8,128)(2,1)}, u32[]{:S(2)}) copy-start(bf16[512,3,128]{2,0,1:T(8,128)(2,1)} %param.13) | copy-start | bytes 1179652
  6.5 186.2 %reduce-scatter.4.cloned.1.call-start = ((), (), s32[]{:S(2)}) async-start(), calls=%async_computation.1 | async-start | bytes 1966080
  6.5 8.0 %collective-permute-start.1 = (bf16[4,384,128]{2,1,0:T(8,128)(2,1)}, bf16[4,384,128]{2,1,0:T(8,128)(2,1)S(1)}, u32[]{:S(2)}, u32[]{:S(2)}) collective-permute-start(bf16[4,384,128]{2,1,0:T(8,128)(2,1)} %param.11), channel_id=1, source_target_pairs={{0,1},{1,2},{2,3},{3,0},{4,5},{5,6},{6,7},{7,4},{8,9},{9,10},{10,1... | collective-permute-start | bytes 1179656 | tf_op jit(solution)/shard_map/ppermute | solution.py:12
  14.6 14.2 %collective-permute-start.2 = (bf16[4,384,128]{2,1,0:T(8,128)(2,1)S(1)}, bf16[4,384,128]{2,1,0:T(8,128)(2,1)S(1)}, u32[]{:S(2)}, u32[]{:S(2)}) collective-permute-start(bf16[4,384,128]{2,1,0:T(8,128)(2,1)S(1)} %collective-permute-done.1), channel_id=1, source_target_pairs={{0,1},{1,2},{2,3},{3,0},{4,5},{5,6},{6,7},{7,4},{8,9},{9,10},{10,1... | collective-permute-start | bytes 1179656 | tf_op jit(solution)/shard_map/ppermute | solution.py:12
  28.8 7.2 %collective-permute-start.3 = (bf16[4,384,128]{2,1,0:T(8,128)(2,1)S(1)}, bf16[4,384,128]{2,1,0:T(8,128)(2,1)S(1)}, u32[]{:S(2)}, u32[]{:S(2)}) collective-permute-start(bf16[4,384,128]{2,1,0:T(8,128)(2,1)S(1)} %collective-permute-done.2), channel_id=1, source_target_pairs={{0,1},{1,2},{2,3},{3,0},{4,5},{5,6},{6,7},{7,4},{8,9},{9,10},{10,1... | collective-permute-start | bytes 1179656 | tf_op jit(solution)/shard_map/ppermute | solution.py:12
  29.6 6.9 %copy-start.5 = (bf16[4,384,128]{2,1,0:T(8,128)(2,1)S(1)}, bf16[4,384,128]{2,1,0:T(8,128)(2,1)}, u32[]{:S(2)}) copy-start(bf16[4,384,128]{2,1,0:T(8,128)(2,1)} %param.11) | copy-start | bytes 1179652
  36.6 1.0 copy-start.10
  37.6 4.8 %copy-start.8 = (f32[3,3,128]{2,1,0:T(4,128)S(1)}, f32[3,3,128]{2,1,0:T(4,128)}, u32[]{:S(2)}) copy-start(f32[3,3,128]{2,1,0:T(4,128)} %param.14) | copy-start | bytes 13828
  38.6 3.8 %copy-start.6 = (bf16[4,384,3,128]{3,1,2,0:T(8,128)(2,1)}, bf16[4,384,3,128]{3,1,2,0:T(8,128)(2,1)S(1)}, u32[]{:S(2)}) copy-start(bf16[4,384,3,128]{3,1,2,0:T(8,128)(2,1)S(1)} %fusion.12) | copy-start | bytes 3538948
  38.7 18.1 %collective-permute-start.4 = (bf16[4,2,3,128]{3,1,2,0:T(2,128)(2,1)S(1)}, bf16[4,2,3,128]{3,1,2,0:T(2,128)(2,1)S(1)}, u32[]{:S(2)}, u32[]{:S(2)}) collective-permute-start(bf16[4,2,3,128]{3,1,2,0:T(2,128)(2,1)S(1)} %slice.56), channel_id=1, source_target_pairs={{0,4},{4,8},{8,12},{1,5},{5,9},{9,13},{2,6},{6,10},{10,14},{3,7},{... | collective-permute-start | bytes 18440 | tf_op jit(solution)/shard_map/ppermute | solution.py:21
  59.0 1.4 copy-start.1
  59.0 4.4 %copy-start.2 = (bf16[4,384,767]{2,1,0:T(8,128)(2,1)S(1)}, bf16[4,384,767]{2,1,0:T(8,128)(2,1)}, u32[]{:S(2)}) copy-start(bf16[4,384,767]{2,1,0:T(8,128)(2,1)} %reshape.40) | copy-start | bytes 7068676
  60.5 4.4 %copy-start.3 = (bf16[4,384,1,128]{3,1,2,0:T(8,128)(2,1)}, bf16[4,384,1,128]{3,1,2,0:T(8,128)(2,1)S(1)}, u32[]{:S(2)}) copy-start(bf16[4,384,1,128]{3,1,2,0:T(8,128)(2,1)S(1)} %fusion.16) | copy-start | bytes 1179652
  64.9 9.9 %collective-permute-start = (bf16[4,384,128]{1,2,0:T(8,128)(2,1)}, bf16[4,384,128]{1,2,0:T(8,128)(2,1)S(1)}, u32[]{:S(2)}, u32[]{:S(2)}) collective-permute-start(bf16[4,384,128]{1,2,0:T(8,128)(2,1)} %get-tuple-element.183), channel_id=1, source_target_pairs={{0,4},{4,8},{8,12},{1,5},{5,9},{9,13},{2,6},{6,10},{10,14},{3,7},{... | collective-permute-start | bytes 1179656 | tf_op jit(solution)/shard_map/while/body/eval_jaxpr/ppermute | solution.py:21
  75.5 30.5 %collective-permute-start = (bf16[4,384,128]{1,2,0:T(8,128)(2,1)}, bf16[4,384,128]{1,2,0:T(8,128)(2,1)S(1)}, u32[]{:S(2)}, u32[]{:S(2)}) collective-permute-start(bf16[4,384,128]{1,2,0:T(8,128)(2,1)} %get-tuple-element.183), channel_id=1, source_target_pairs={{0,4},{4,8},{8,12},{1,5},{5,9},{9,13},{2,6},{6,10},{10,14},{3,7},{... | collective-permute-start | bytes 1179656 | tf_op jit(solution)/shard_map/while/body/eval_jaxpr/ppermute | solution.py:21
  106.8 10.3 %collective-permute-start = (bf16[4,384,128]{1,2,0:T(8,128)(2,1)}, bf16[4,384,128]{1,2,0:T(8,128)(2,1)S(1)}, u32[]{:S(2)}, u32[]{:S(2)}) collective-permute-start(bf16[4,384,128]{1,2,0:T(8,128)(2,1)} %get-tuple-element.183), channel_id=1, source_target_pairs={{0,4},{4,8},{8,12},{1,5},{5,9},{9,13},{2,6},{6,10},{10,14},{3,7},{... | collective-permute-start | bytes 1179656 | tf_op jit(solution)/shard_map/while/body/eval_jaxpr/ppermute | solution.py:21
  117.8 2.4 %copy-start.4 = (bf16[4,384,1,128]{3,1,2,0:T(8,128)(2,1)S(1)}, bf16[4,384,1,128]{3,1,2,0:T(8,128)(2,1)}, u32[]{:S(2)}) copy-start(bf16[4,384,1,128]{3,1,2,0:T(8,128)(2,1)} %copy-done.3) | copy-start | bytes 1179652
  117.8 2.4 %copy-start.7 = (bf16[128,512]{1,0:T(8,128)(2,1)S(1)}, bf16[128,512]{1,0:T(8,128)(2,1)}, u32[]{:S(2)}) copy-start(bf16[128,512]{1,0:T(8,128)(2,1)} %param.17) | copy-start | bytes 393220
  117.8 2.4 %copy-start.9 = (f32[128]{0:T(128)S(1)}, f32[128]{0:T(128)}, u32[]{:S(2)}) copy-start(f32[128]{0:T(128)} %param.16) | copy-start | bytes 1540
Sparse Core Ops, SparseCore 0:
  125.2 67.4 reduce-scatter.3
